TPU v7x, 512 devices: a whole 4x4x16 slice. The times are simulated.
512 devices in a mesh: seq: 32 (over z, core), hid: 16 (over x, y).
Axes of the slice: x: 4, y: 4, z: 16, core: 2. Of those that a mesh axis runs over, the one named last changes fastest.
Arguments:
- activations: bfloat16 [16384, 4096], P('seq'), may hold values from -6 to 6
- w_inner: bfloat16 [4096, 4096], P('seq', 'hid'), may hold values from -0.09375 to 0.09375
- w_gate: bfloat16 [4096, 4096], P('seq', 'hid'), may hold values from -0.09375 to 0.09375
- w_groups: bfloat16 [4096, 1024], P('seq'), may hold values from -0.09375 to 0.09375
- w_step: bfloat16 [4096, 64], P('seq'), may hold values from -0.09375 to 0.09375
- w_out: bfloat16 [4096, 4096], P('seq', 'hid'), may hold values from -0.09375 to 0.09375
- conv_inner: float32 [4, 4096], P(None, 'hid'), may hold values from -3 to 3
- conv_groups: float32 [4, 1024], replicated, may hold values from -3 to 3
- step_bias: float32 [64], P('hid'), may hold values from -4 to 0
- decay_log: float32 [64], P('hid'), may hold values from -9 to -1
- skip_gain: float32 [64], P('hid'), may hold values from 0.5 to 1.5
- norm_gain: float32 [4096], P('hid'), may hold values from 0.5 to 1.5
Outputs:
- layer_out: bfloat16 [16384, 4096], P('seq', 'hid')
All inputs are finite; a program needn't handle non-finite values.
Results may differ from a plain program's by a relative error of at most 0.02.
Values may be sent and summed in bfloat16 or wider, within the bound.
A program may use at most 64 MiB of HBM per device.

v0:
```python
import jax
import jax.numpy as jnp
from jax import lax
from jax.sharding import PartitionSpec as P

HEADS = 64
P_SIZE = 64
N = 128
G = 4
Q = 256
K = 4
INNER = 4096


def from_behind(block, axis, distance):
    devices = range(lax.axis_size(axis))
    route = [(i - distance, i) for i in devices if i - distance in devices]
    return lax.ppermute(block, axis, route)


def carried_in(array, axis, join, neutral):
    place = lax.axis_index(axis)
    gathered = jax.tree.map(
        lambda a, kind: lax.all_gather(a.astype(kind), axis), array, (jnp.bfloat16, jnp.bfloat16)
    )
    state = jax.tree.map(lambda a, e: jnp.zeros_like(a) + jnp.asarray(e, a.dtype), array, neutral)

    def one(step, state):
        return join(
            state,
            jax.tree.map(
                lambda a, own: lax.dynamic_index_in_dim(a, step, 0, False).astype(own.dtype),
                gathered,
                array,
            ),
        )

    return lax.fori_loop(0, place, one, state)


def causal_conv(values, before, kernel):
    length = values.shape[0]
    extended = jnp.concatenate([before, values], axis=0)
    summed = jnp.zeros(values.shape, jnp.float32)
    for position in range(kernel.shape[0]):
        summed = (
            summed + extended[position : position + length].astype(jnp.float32) * kernel[position]
        )
    return jax.nn.silu(summed).astype(jnp.bfloat16)


def combine_states(earlier, later):
    return (earlier[0] * later[0], later[0][:, None, None] * earlier[1] + later[1])


def roll_state(state, inputs):
    total_here, fresh_here = inputs
    return (jnp.exp(total_here)[:, None, None] * state + fresh_here, state)


def local(
    activations,
    w_inner,
    w_gate,
    w_groups,
    w_step,
    w_out,
    conv_inner,
    conv_groups,
    step_bias,
    decay_log,
    skip_gain,
    norm_gain,
):
    tok_rows = activations.shape[0]
    heads_dev = step_bias.shape[0]
    width_dev = w_inner.shape[1]
    head_block = lax.axis_index("hid")
    group_cols = 2 * N
    group_index = head_block * heads_dev // (HEADS // G)
    step_cols = lax.dynamic_slice_in_dim(w_step, head_block * heads_dev, heads_dev, 1)
    own_cols = lax.dynamic_slice_in_dim(w_groups, group_index * group_cols, group_cols, 1)
    piece_inner = lax.all_gather(w_inner, "seq", axis=0, tiled=True)
    piece_gate = lax.all_gather(w_gate, "seq", axis=0, tiled=True)
    piece_groups = lax.all_gather(own_cols, "seq", axis=0, tiled=True)
    piece_step = lax.all_gather(step_cols, "seq", axis=0, tiled=True)
    piece_out = lax.all_gather(w_out, "seq", axis=0, tiled=True)
    acc_inner = jnp.dot(activations, piece_inner, preferred_element_type=jnp.float32)
    acc_gate = jnp.dot(activations, piece_gate, preferred_element_type=jnp.float32)
    acc_groups = jnp.dot(activations, piece_groups, preferred_element_type=jnp.float32)
    acc_step = jnp.dot(activations, piece_step, preferred_element_type=jnp.float32)
    groups_in = acc_groups.astype(jnp.bfloat16)
    inner_in = acc_inner.astype(jnp.bfloat16)
    gate_in = acc_gate.astype(jnp.bfloat16)
    conv_group = lax.dynamic_slice_in_dim(conv_groups, group_index * group_cols, group_cols, 1)
    tail_rows = K - 1
    inner_prev, groups_prev = from_behind(
        (inner_in[tok_rows - tail_rows :], groups_in[tok_rows - tail_rows :]), "seq", 1
    )
    inner_conv = causal_conv(inner_in, inner_prev, conv_inner)
    groups_conv = causal_conv(groups_in, groups_prev, conv_group)
    step_size = jax.nn.softplus(acc_step + step_bias)
    rates = -jnp.exp(decay_log)
    span_count = tok_rows // Q
    heads_x = inner_conv.reshape(span_count, Q, heads_dev, P_SIZE)
    b_in = groups_conv[:, :N].reshape(span_count, Q, N)
    c_out = groups_conv[:, N:].reshape(span_count, Q, N)
    block_dt = step_size.reshape(span_count, Q, heads_dev)
    cum_decay = jnp.cumsum(block_dt * rates, axis=1)
    scores = jnp.einsum("ctn,csn->cts", c_out, b_in, preferred_element_type=jnp.float32)
    ahead = jnp.arange(Q)[:, None] >= jnp.arange(Q)[None, :]
    decay_t = jnp.swapaxes(cum_decay, 1, 2)
    gap = jnp.where(ahead, decay_t[:, :, :, None] - decay_t[:, :, None, :], -1e30)
    mixing = (scores[:, None] * jnp.exp(gap) * jnp.swapaxes(block_dt, 1, 2)[:, :, None, :]).astype(
        jnp.bfloat16
    )
    intra = jnp.einsum("chts,cshp->cthp", mixing, heads_x, preferred_element_type=jnp.float32)
    span_total = cum_decay[:, -1]
    weights_in = jnp.exp(span_total[:, None, :] - cum_decay) * block_dt
    weighted = (b_in[:, :, None, :] * weights_in[:, :, :, None]).astype(jnp.bfloat16)
    fresh = jnp.einsum("cshn,cshp->chnp", weighted, heads_x, preferred_element_type=jnp.float32)
    zero_state = jnp.zeros((heads_dev, N, P_SIZE), jnp.float32)
    local_end, starts = lax.scan(roll_state, zero_state, (span_total, fresh))
    log_total = jnp.sum(span_total, axis=0)
    prior = jnp.cumsum(span_total, axis=0) - span_total
    identity = (jnp.ones((heads_dev,), jnp.float32), zero_state)
    state_in = carried_in((jnp.exp(log_total), local_end), "seq", combine_states, identity)[1]
    span_in = starts + jnp.exp(prior)[:, :, None, None] * state_in[None]
    inter = jnp.einsum(
        "ctn,chnp->cthp", c_out.astype(jnp.float32), span_in, precision=lax.Precision.HIGHEST
    )
    inter = inter * jnp.exp(cum_decay)[:, :, :, None]
    mixed = (intra + inter).reshape(tok_rows, width_dev) + jnp.repeat(
        skip_gain, P_SIZE
    ) * inner_conv.astype(jnp.float32)
    gated = mixed * jax.nn.silu(gate_in.astype(jnp.float32))
    squares = lax.psum(jnp.sum(gated * gated, axis=1), "hid")
    normed = (gated * lax.rsqrt(squares / INNER + 1e-05)[:, None] * norm_gain).astype(jnp.bfloat16)
    terms = lax.dot_general(
        normed, piece_out, (((1,), (1,)), ((), ())), preferred_element_type=jnp.float32
    )
    return lax.psum_scatter(terms.astype(jnp.bfloat16), "hid", scatter_dimension=1, tiled=True)


def solution(mesh):
    in_specs = (
        P("seq", None),
        P("seq", "hid"),
        P("seq", "hid"),
        P("seq", None),
        P("seq", None),
        P("seq", "hid"),
        P(None, "hid"),
        P(),
        P("hid"),
        P("hid"),
        P("hid"),
        P("hid"),
    )
    out_specs = P("seq", "hid")
    return jax.shard_map(local, mesh=mesh, in_specs=in_specs, out_specs=out_specs, check_vma=False)
```

profile of v0, /device:TPU:32, one launch (start us, length us, event | category | flops | bytes accessed | tf_op | source)
XLA Modules:
  0.0 480.8 jit_solution(4946631433308588536)
XLA Ops:
  6.5 0.9 copy-done
  7.5 0.6 constant_dynamic-slice_fusion.4
  8.2 0.7 all-gather.8.cloned.1.call-update
  9.0 0.7 constant_dynamic-slice_fusion.3
  9.7 34.2 %all_gather.27 = bf16[4096,4]{0,1:T(4,128)(2,1)S(1)} all-gather(bf16[128,4]{0,1:T(4,128)(2,1)S(1)} %constant_dynamic-slice_fusion.3), channel_id=1, replica_groups=mesh['seq'=32,'hid'=16] {'seq'}, dimensions={0}, use_global_device_ids=true | all-gather | bytes 33792 | tf_op jit(solution)/shard_map/all_gather | solution.py:86
  43.8 0.7 exponential_negate_fusion
  44.5 3.5 compare_select_fusion
  48.1 2.4 reduce-window.6
  50.9 0.9 constant_dynamic-slice_fusion.2
  52.1 32.9 %all-gather.10.cloned.1.call-done = bf16[4096,256]{1,0:T(8,128)(2,1)} async-done(((bf16[128,256]{1,0:T(8,128)(2,1)}), bf16[4096,256]{1,0:T(8,128)(2,1)}) %all-gather.10.cloned.1.call-update) | async-done | bytes 2097168 | tf_op jit(solution)/shard_map/all_gather | solution.py:85
  85.0 4.1 fusion.4
  89.2 2.1 collective-permute-start.1
  91.3 64.3 %all-gather.8.cloned.1.call-done = bf16[4096,256]{1,0:T(8,128)(2,1)} async-done(((bf16[128,256]{1,0:T(8,128)(2,1)}), bf16[4096,256]{1,0:T(8,128)(2,1)}) %all-gather.8.cloned.1.call-update) | async-done | bytes 2097168 | tf_op jit(solution)/shard_map/all_gather | solution.py:83
  155.6 4.1 convolution_convert_fusion.3
  159.8 2.1 collective-permute-start
  162.3 2.3 collective-permute-done
  165.5 0.8 fusion.12
  166.7 0.7 copy.84
  168.7 1.3 dynamic-slice
  170.9 44.1 %all-reduce = bf16[128]{0:T(256)(128)(2,1)S(1)} all-reduce(bf16[128]{0:T(256)(128)(2,1)S(1)} %dynamic-update-slice), channel_id=2, replica_groups=mesh['seq'=32,'hid'=16] {'seq'}, use_global_device_ids=true, to_apply=%add | all-reduce | flops 128 | bytes 512
  215.5 21.5 %all-gather.16.cloned.1.call-done = bf16[128,128,64]{1,2,0:T(8,128)(2,1)} async-done(((bf16[4,128,64]{1,2,0:T(8,128)(2,1)}), bf16[128,128,64]{1,2,0:T(8,128)(2,1)}) %all-gather.16.cloned.1.call-update) | async-done | bytes 2097168 | tf_op jit(solution)/shard_map/all_gather | solution.py:24
  237.1 2.3 while.25
  237.1 0.9 constant_dynamic-slice_fusion.6
  238.2 0.9 constant_dynamic-slice_fusion.6
  240.1 0.8 fusion.2
  241.2 0.6 reshape.121
  241.8 65.7 %all-gather.12.cloned.1.call-done = bf16[4096,256]{1,0:T(8,128)(2,1)} async-done(((bf16[128,256]{1,0:T(8,128)(2,1)}), bf16[4096,256]{1,0:T(8,128)(2,1)}) %all-gather.12.cloned.1.call-update) | async-done | bytes 2097168 | tf_op jit(solution)/shard_map/all_gather | solution.py:84
  307.5 4.3 multiply_reduce_fusion
  311.8 40.3 %psum.7 = f32[512]{0:T(512)S(1)} all-reduce(f32[512]{0:T(512)S(1)} %get-tuple-element.172), channel_id=1, replica_groups=mesh['seq'=32,'hid'=16] {'hid'}, use_global_device_ids=true, to_apply=%region_9.10 | all-reduce | flops 512 | bytes 4096 | tf_op jit(solution)/shard_map/psum | solution.py:137
  352.1 25.9 %all-gather.14.cloned.1.call-done = bf16[4096,256]{1,0:T(8,128)(2,1)} async-done(((bf16[128,256]{1,0:T(8,128)(2,1)}), bf16[4096,256]{1,0:T(8,128)(2,1)}) %all-gather.14.cloned.1.call-update) | async-done | bytes 2097168 | tf_op jit(solution)/shard_map/all_gather | solution.py:87
  378.0 4.8 %convolution_convert_fusion = bf16[512,4096]{1,0:T(8,128)(2,1)} fusion(bf16[4096,256]{1,0:T(8,128)(2,1)} %all-gather.14.cloned.1.call-done, f32[512,256]{1,0:T(8,128)S(1)} %get-tuple-element.173, f32[256]{0:T(256)S(1)} %copy-done.1, f32[512]{0:T(512)S(1)} %add_rsqrt_fusion), kind=kOutput, calls=%fused_computation.8 | convolution fusion | flops 1076232192 | bytes 6818816 | tf_op jit(solution)/shard_map/dot_general | solution.py:139
  382.9 91.1 %reduce-scatter.2.cloned.1.call-done = bf16[512,256]{1,0:T(8,128)(2,1)} async-done(((bf16[512,4096]{1,0:T(8,128)(2,1)}), bf16[512,256]{1,0:T(8,128)(2,1)}) %reduce-scatter.2.cloned.1.call-update) | async-done | bytes 262160 | tf_op jit(solution)/shard_map/reduce_scatter | solution.py:142
  (70 shorter events, 6.4 us)
Async XLA Ops:
  6.5 1.0 copy-start
  6.5 78.5 %all-gather.10.cloned.1.call-start = ((), (), s32[]{:S(2)}) async-start(), calls=%async_computation.2 | async-start | bytes 2162688 | tf_op jit(solution)/shard_map/all_gather | solution.py:85
  8.1 147.5 %all-gather.8.cloned.1.call-start = ((), (), s32[]{:S(2)}) async-start(), calls=%async_computation.1 | async-start | bytes 2162688 | tf_op jit(solution)/shard_map/all_gather | solution.py:83
  8.9 228.1 %all-gather.16.cloned.1.call-start = ((), (), s32[]{:S(2)}) async-start(), calls=%async_computation.6 | async-start | bytes 2162688 | tf_op jit(solution)/shard_map/all_gather | solution.py:24
  44.5 7.5 %copy-start.2 = (f32[4,256]{1,0:T(4,128)S(1)}, f32[4,256]{1,0:T(4,128)}, u32[]{:S(2)}) copy-start(f32[4,256]{1,0:T(4,128)} %param.22) | copy-start | bytes 12292
  89.2 72.7 %collective-permute-start.1 = (bf16[3,256]{1,0:T(4,128)(2,1)S(1)}, bf16[3,256]{1,0:T(4,128)(2,1)S(1)}, u32[]{:S(2)}, u32[]{:S(2)}) collective-permute-start(bf16[3,256]{1,0:T(4,128)(2,1)S(1)} %slice.89), channel_id=1, source_target_pairs={{0,16},{16,32},{32,48},{48,64},{64,80},{80,96},{96,112},{112,128},... | collective-permute-start | bytes 4616 | tf_op jit(solution)/shard_map/ppermute | solution.py:18
  159.8 4.9 %collective-permute-start = (bf16[3,256]{1,0:T(4,128)(2,1)S(1)}, bf16[3,256]{1,0:T(4,128)(2,1)S(1)}, u32[]{:S(2)}, u32[]{:S(2)}) collective-permute-start(bf16[3,256]{1,0:T(4,128)(2,1)S(1)} %slice.84), channel_id=1, source_target_pairs={{0,16},{16,32},{32,48},{48,64},{64,80},{80,96},{96,112},{112,128},... | collective-permute-start | bytes 4616 | tf_op jit(solution)/shard_map/ppermute | solution.py:18
  166.3 48.7 %copy-start.3 = (f32[4]{0:T(128)S(1)}, f32[4]{0:T(128)}, u32[]{:S(2)}) copy-start(f32[4]{0:T(128)} %param.26) | copy-start | bytes 52
  167.4 140.1 %all-gather.12.cloned.1.call-start = ((), (), s32[]{:S(2)}) async-start(), calls=%async_computation.3 | async-start | bytes 2162688 | tf_op jit(solution)/shard_map/all_gather | solution.py:84
  168.0 210.0 %all-gather.14.cloned.1.call-start = ((), (), s32[]{:S(2)}) async-start(), calls=%async_computation.4 | async-start | bytes 2162688 | tf_op jit(solution)/shard_map/all_gather | solution.py:87
  168.6 305.3 %reduce-scatter.2.cloned.1.call-start = ((), (), s32[]{:S(2)}) async-start(), calls=%async_computation.5 | async-start | bytes 4456448 | tf_op jit(solution)/shard_map/reduce_scatter | solution.py:142
  241.8 136.2 %copy-start.1 = (f32[256]{0:T(256)S(1)}, f32[256]{0:T(256)}, u32[]{:S(2)}) copy-start(f32[256]{0:T(256)} %param.27) | copy-start | bytes 3076
Sparse Core Ops, SparseCore 0:
  9.5 75.5 all-gather.9
  87.1 68.4 all-gather.7
  167.5 69.4 all-gather.15
  239.0 68.4 all-gather.11
  309.5 68.4 all-gather.13
  383.0 90.8 reduce-scatter.1
where the time goes:
time: 483 us; the launch traced here: 481 us
  waiting for transfers between devices  306 us (63%)
  blocking collectives  119 us (25%)
  matrix products  22.9 us (5%)
  between operations  14.4 us (3%)
  local copies, waits for them, and re-layouts  9.82 us (2%)
  other arithmetic  4.96 us (1%)
    reduce_scatter x1, waiting for transfers between devices, local(): lax.psum_scatter(terms.astype(jnp.bfloat16), 'hid', scatter_dimension=1,...  91.1 us
    all_gather x1, waiting for transfers between devices, local(): piece_gate = lax.all_gather(w_gate, 'seq', axis=0, tiled=True)  65.7 us
    all_gather x1, waiting for transfers between devices, local(): piece_inner = lax.all_gather(w_inner, 'seq', axis=0, tiled=True)  64.3 us
    unnamed x1, blocking collectives  44.1 us
    psum x1, blocking collectives, local(): squares = lax.psum(jnp.sum(gated * gated, axis=1), 'hid')  40.3 us
    all_gather x1, blocking collectives, local(): piece_step = lax.all_gather(step_cols, 'seq', axis=0, tiled=True)  34.2 us
    all_gather x1, waiting for transfers between devices, local(): piece_groups = lax.all_gather(own_cols, 'seq', axis=0, tiled=True)  32.9 us
    all_gather x1, waiting for transfers between devices, local(): piece_out = lax.all_gather(w_out, 'seq', axis=0, tiled=True)  25.9 us
  transfers between devices with their start and end apart: 8, of which 7 were waited for; matrix products, arithmetic and copies ran while one was open for 6% of the time, Pallas kernels for 0%

commit v1 on v0

--- a/solution.py
+++ b/solution.py
@@ -84,7 +84,15 @@
     piece_gate = lax.all_gather(w_gate, "seq", axis=0, tiled=True)
     piece_groups = lax.all_gather(own_cols, "seq", axis=0, tiled=True)
     piece_step = lax.all_gather(step_cols, "seq", axis=0, tiled=True)
-    piece_out = lax.all_gather(w_out, "seq", axis=0, tiled=True)
+    piece_out = jnp.concatenate(
+        jax.lax.all_to_all(
+            jnp.stack([w_out] * jax.lax.psum(1, axis_name="seq")),
+            axis_name="seq",
+            split_axis=0,
+            concat_axis=0,
+        ),
+        axis=0,
+    )
     acc_inner = jnp.dot(activations, piece_inner, preferred_element_type=jnp.float32)
     acc_gate = jnp.dot(activations, piece_gate, preferred_element_type=jnp.float32)
     acc_groups = jnp.dot(activations, piece_groups, preferred_element_type=jnp.float32)

time: 483 us -> 505 us (1.046)
  blocking collectives: 119 us -> 210 us
  waiting for transfers between devices: 306 us -> 219 us
  starting transfers between devices: 4.46 us -> 14.3 us
    unnamed x1, blocking collectives: 44.1 us -> 136 us
    all_gather x1, waiting for transfers between devices: 65.7 us -> 16 us  [local(): piece_gate = lax.all_gather(w_gate, 'seq', axis=0, tiled=True)]
    all_gather x1 -> x0, waiting for transfers between devices: 25.9 us -> none  [local(): piece_out = lax.all_gather(w_out, 'seq', axis=0, tiled=True)]
    all_gather x1, waiting for transfers between devices: 21.5 us -> 0.01 us  [carried_in(): lax.all_gather(a.astype(kind), axis)]
    reduce_scatter x1, waiting for transfers between devices: 91.1 us -> 103 us  [local(): lax.psum_scatter(terms.astype(jnp.bfloat16), 'hid', scatter_dimension=1,...]
    all_to_all x0 -> x1, starting transfers between devices: none -> 9.83 us  [local(): jax.lax.all_to_all(jnp.stack([w_out] * jax.lax.psum(1, axis_name='seq')),...]
  transfers between devices with their start and end apart: 8 -> 8, of which waited for: 7 -> 5; matrix products, arithmetic and copies ran while one was open for 6% -> 8% of each run, Pallas kernels for 0% -> 0%
where the time goes in v1:
time: 505 us; the launch traced here: 503 us
  waiting for transfers between devices  219 us (43%)
  blocking collectives  210 us (42%)
  matrix products  24.1 us (5%)
  starting transfers between devices  14.3 us (3%)
  between operations  14 us (3%)
  local copies, waits for them, and re-layouts  13.9 us (3%)
  other arithmetic  7.7 us (2%)
    unnamed x1, blocking collectives  136 us
    reduce_scatter x1, waiting for transfers between devices, local(): lax.psum_scatter(terms.astype(jnp.bfloat16), 'hid', scatter_dimension=1,...  103 us
    all_gather x1, waiting for transfers between devices, local(): piece_inner = lax.all_gather(w_inner, 'seq', axis=0, tiled=True)  64.3 us
    psum x1, blocking collectives, local(): squares = lax.psum(jnp.sum(gated * gated, axis=1), 'hid')  40.3 us
    all_gather x1, blocking collectives, local(): piece_step = lax.all_gather(step_cols, 'seq', axis=0, tiled=True)  34.2 us
    all_gather x1, waiting for transfers between devices, local(): piece_groups = lax.all_gather(own_cols, 'seq', axis=0, tiled=True)  32.4 us
    all_gather x1, waiting for transfers between devices, local(): piece_gate = lax.all_gather(w_gate, 'seq', axis=0, tiled=True)  16 us
  transfers between devices with their start and end apart: 8, of which 5 were waited for; matrix products, arithmetic and copies ran while one was open for 8% of the time, Pallas kernels for 0%

profile of v1, /device:TPU:32, one launch (start us, length us, event | category | flops | bytes accessed | tf_op | source)
XLA Modules:
  0.0 503.0 jit_solution(7831252039685737083)
XLA Ops:
  6.5 0.9 copy-done
  8.2 0.7 all-gather.7.cloned.1.call-update
  9.7 34.2 %all_gather.24 = bf16[4096,4]{0,1:T(4,128)(2,1)S(1)} all-gather(bf16[128,4]{0,1:T(4,128)(2,1)S(1)} %constant_dynamic-slice_fusion.3), channel_id=1, replica_groups=mesh['seq'=32,'hid'=16] {'seq'}, dimensions={0}, use_global_device_ids=true | all-gather | bytes 33792 | tf_op jit(solution)/shard_map/all_gather | solution.py:86
  44.5 3.5 compare_select_fusion
  48.1 2.4 reduce-window.6
  50.9 0.9 constant_dynamic-slice_fusion.2
  52.7 32.4 %all-gather.9.cloned.1.call-done = bf16[4096,256]{1,0:T(8,128)(2,1)} async-done(((bf16[128,256]{1,0:T(8,128)(2,1)}), bf16[4096,256]{1,0:T(8,128)(2,1)}) %all-gather.9.cloned.1.call-update) | async-done | bytes 2097168 | tf_op jit(solution)/shard_map/all_gather | solution.py:85
  85.0 4.1 fusion.4
  89.2 2.1 collective-permute-start.1
  91.3 64.3 %all-gather.7.cloned.1.call-done = bf16[4096,256]{1,0:T(8,128)(2,1)} async-done(((bf16[128,256]{1,0:T(8,128)(2,1)}), bf16[4096,256]{1,0:T(8,128)(2,1)}) %all-gather.7.cloned.1.call-update) | async-done | bytes 2097168 | tf_op jit(solution)/shard_map/all_gather | solution.py:83
  155.6 4.1 convolution_convert_fusion.3
  159.8 2.1 collective-permute-start
  162.3 2.3 collective-permute-done
  165.5 0.8 fusion.12
  166.7 0.8 copy.84
  167.6 1.6 stack.2
  169.1 9.8 %all-to-all-start = ((bf16[32,128,256]{2,1,0:T(8,128)(2,1)}), bf16[32,128,256]{2,1,0:T(8,128)(2,1)S(1)}, u32[]{:S(2)}, u32[]{:S(2)}) async-start(bf16[32,128,256]{2,1,0:T(8,128)(2,1)} %stack.2), calls=%async_computation | async-start | bytes 4194304 | tf_op jit(solution)/shard_map/all_to_all | solution.py:88
  180.3 1.3 dynamic-slice
  182.5 135.6 %all-reduce = bf16[128]{0:T(256)(128)(2,1)S(1)} all-reduce(bf16[128]{0:T(256)(128)(2,1)S(1)} %dynamic-update-slice), channel_id=2, replica_groups=mesh['seq'=32,'hid'=16] {'seq'}, use_global_device_ids=true, to_apply=%add | all-reduce | flops 128 | bytes 512
  319.4 1.0 fusion.24
  320.5 2.3 while.25
  320.5 0.9 constant_dynamic-slice_fusion.6
  321.7 0.9 constant_dynamic-slice_fusion.6
  322.8 1.2 multiply_add_fusion
  324.5 2.7 fusion.2
  327.2 1.4 copy.93
  328.6 1.4 reshape.127
  330.0 16.0 %all-gather.11.cloned.1.call-done = bf16[4096,256]{1,0:T(8,128)(2,1)} async-done(((bf16[128,256]{1,0:T(8,128)(2,1)}), bf16[4096,256]{1,0:T(8,128)(2,1)}) %all-gather.11.cloned.1.call-update) | async-done | bytes 2097168 | tf_op jit(solution)/shard_map/all_gather | solution.py:84
  346.0 4.3 multiply_reduce_fusion
  350.3 40.3 %psum.7 = f32[512]{0:T(512)S(1)} all-reduce(f32[512]{0:T(512)S(1)} %get-tuple-element.172), channel_id=1, replica_groups=mesh['seq'=32,'hid'=16] {'hid'}, use_global_device_ids=true, to_apply=%region_9.10 | all-reduce | flops 512 | bytes 4096 | tf_op jit(solution)/shard_map/psum | solution.py:145
  390.7 3.2 convolution_convert_fusion
  393.9 102.5 %reduce-scatter.2.cloned.1.call-done = bf16[512,256]{1,0:T(8,128)(2,1)} async-done(((bf16[512,4096]{1,0:T(8,128)(2,1)}), bf16[512,256]{1,0:T(8,128)(2,1)}) %reduce-scatter.2.cloned.1.call-update) | async-done | bytes 262160 | tf_op jit(solution)/shard_map/reduce_scatter | solution.py:150
  (78 shorter events, 9.3 us)
Async XLA Ops:
  6.5 1.0 copy-start
  6.5 78.5 %all-gather.9.cloned.1.call-start = ((), (), s32[]{:S(2)}) async-start(), calls=%async_computation.3 | async-start | bytes 2162688 | tf_op jit(solution)/shard_map/all_gather | solution.py:85
  8.1 147.5 %all-gather.7.cloned.1.call-start = ((), (), s32[]{:S(2)}) async-start(), calls=%async_computation.2 | async-start | bytes 2162688 | tf_op jit(solution)/shard_map/all_gather | solution.py:83
  8.9 311.6 %all-gather.13.cloned.1.call-start = ((), (), s32[]{:S(2)}) async-start(), calls=%async_computation.6 | async-start | bytes 2162688 | tf_op jit(solution)/shard_map/all_gather | solution.py:24
  44.5 7.5 %copy-start.5 = (f32[4,256]{1,0:T(4,128)S(1)}, f32[4,256]{1,0:T(4,128)}, u32[]{:S(2)}) copy-start(f32[4,256]{1,0:T(4,128)} %param.22) | copy-start | bytes 12292
  89.2 72.7 %collective-permute-start.1 = (bf16[3,256]{1,0:T(4,128)(2,1)S(1)}, bf16[3,256]{1,0:T(4,128)(2,1)S(1)}, u32[]{:S(2)}, u32[]{:S(2)}) collective-permute-start(bf16[3,256]{1,0:T(4,128)(2,1)S(1)} %slice.89), channel_id=1, source_target_pairs={{0,16},{16,32},{32,48},{48,64},{64,80},{80,96},{96,112},{112,128},... | collective-permute-start | bytes 4616 | tf_op jit(solution)/shard_map/ppermute | solution.py:18
  159.8 4.9 collective-permute-start
  165.0 4.1 copy-start.1
  166.3 1.2 copy-start.3
  166.7 2.5 copy-start.2
  169.1 10.5 %copy-start.7 = (f32[4]{0:T(128)S(1)}, f32[4]{0:T(128)}, u32[]{:S(2)}) copy-start(f32[4]{0:T(128)} %param.26) | copy-start | bytes 52
  169.1 221.5 %all-to-all-start = ((bf16[32,128,256]{2,1,0:T(8,128)(2,1)}), bf16[32,128,256]{2,1,0:T(8,128)(2,1)S(1)}, u32[]{:S(2)}, u32[]{:S(2)}) async-start(bf16[32,128,256]{2,1,0:T(8,128)(2,1)} %stack.2), calls=%async_computation | async-start | bytes 4194304 | tf_op jit(solution)/shard_map/all_to_all | solution.py:88
  179.0 167.0 %all-gather.11.cloned.1.call-start = ((), (), s32[]{:S(2)}) async-start(), calls=%async_computation.4 | async-start | bytes 2162688 | tf_op jit(solution)/shard_map/all_gather | solution.py:84
  179.6 316.9 %reduce-scatter.2.cloned.1.call-start = ((), (), s32[]{:S(2)}) async-start(), calls=%async_computation.5 | async-start | bytes 4456448 | tf_op jit(solution)/shard_map/reduce_scatter | solution.py:150
  327.2 18.8 %copy-start.6 = (f32[256]{0:T(256)S(1)}, f32[256]{0:T(256)}, u32[]{:S(2)}) copy-start(f32[256]{0:T(256)} %mul.255) | copy-start | bytes 3076
  330.0 60.6 %copy-start.4 = (f32[256]{0:T(256)S(1)}, f32[256]{0:T(256)}, u32[]{:S(2)}) copy-start(f32[256]{0:T(256)} %param.27) | copy-start | bytes 3076
Sparse Core Ops, SparseCore 0:
  9.5 75.5 all-gather.8
  87.1 68.4 all-gather.6
  167.7 97.8 all-gather.12
  267.5 78.4 all-gather.10
  394.0 102.3 reduce-scatter.1
